TPU v7x, 256 devices: a whole 4x4x8 slice. The times are simulated.
256 devices in a mesh: space: 8 (over z), tm: 16 (over y, x), param: 2 (over core).
Axes of the slice: x: 4, y: 4, z: 8, core: 2. Of those that a mesh axis runs over, the one named last changes fastest.
Arguments:
- snapshots: float32 [512, 64, 6144], P('tm', 'param', 'space'), may hold values from -6 to 6
- time_basis: float32 [512, 64], replicated, may hold values from -0.25 to 0.25
Outputs:
- gram_time: float32 [512, 512], P('tm')
- core: float32 [64, 64, 6144], P('tm', 'param', 'space')
- gram_param: float32 [64, 64], P('param')
All inputs are finite; a program needn't handle non-finite values.
Results may differ from a plain program's by a relative error of at most 0.000071.
Values sent between devices are 32-bit elements; how exact they have to be, the bound alone decides.
A program may use at most 128 MiB of HBM per device.

v0:
```python
import jax
import jax.numpy as jnp
from jax import lax
from jax.sharding import PartitionSpec as P

precise_mode = lax.Precision.HIGHEST


def body(snapshots, time_basis):
    time_local, load_local, point_local = snapshots.shape
    total_points = point_local * lax.axis_size("space")
    all_loads = load_local * lax.axis_size("param")
    rank_all = time_basis.shape[1]
    traded = lax.all_to_all(snapshots, "tm", split_axis=2, concat_axis=0, tiled=True)
    rows_part = lax.psum_scatter(
        jnp.einsum("tps,ups->tu", traded, traded, precision=precise_mode),
        "tm",
        scatter_dimension=0,
        tiled=True,
    )
    gram_time = lax.psum(rows_part, ("space", "param")) / (all_loads * total_points)
    basis_rows = lax.dynamic_slice_in_dim(
        time_basis, lax.axis_index("tm") * time_local, time_local, 0
    )
    core = lax.psum_scatter(
        jnp.einsum("tr,tps->rps", basis_rows, snapshots, precision=precise_mode),
        "tm",
        scatter_dimension=0,
        tiled=True,
    )
    param_part = jnp.einsum(
        "rps,rqs->pq",
        core,
        lax.all_gather(core, "param", axis=1, tiled=True),
        precision=precise_mode,
    )
    gram_param = lax.psum(param_part, ("space", "tm")) / (rank_all * total_points)
    return (gram_time, core, gram_param)


def solution(mesh):
    placed = (P("tm", "param", "space"), P())
    return jax.shard_map(
        body,
        mesh=mesh,
        in_specs=placed,
        out_specs=(P("tm", None), P("tm", "param", "space"), P("param", None)),
        check_vma=False,
    )
```

profile of v0, /device:TPU:0, one launch (start us, length us, event | category | flops | bytes accessed | tf_op | source)
XLA Modules:
  0.0 1105.7 jit_solution(3730888095807940224)
XLA Ops:
  7.2 0.0 copy-start
  7.2 0.0 reduce-scatter.3.cloned.1.call-start
  7.2 11.3 %copy.17 = f32[32,32,768]{1,0,2:T(8,128)} copy(f32[32,32,768]{2,1,0:T(8,128)} %param.2) | data formatting | bytes 6291456 | tf_op args[0]
  18.6 14.1 %reshape.9 = f32[16,1,49152]{2,1,0:T(1,128)} reshape(f32[768,32,32]{2,1,0:T(8,128)} %bitcast.21) | data formatting | bytes 6291456
  32.7 44.9 %all_to_all.18 = f32[16,1,49152]{2,1,0:T(1,128)S(1)} all-to-all(f32[16,1,49152]{2,1,0:T(1,128)} %reshape.9), channel_id=1, replica_groups=mesh['space'=8,'tm'=16,'param'=2] {'tm'}, dimensions={0} | all-to-all | bytes 6291456 | tf_op jit(solution)/shard_map/all_to_all | solution.py:14
  77.6 0.5 broadcast.2
  78.1 10.8 reduce
  88.9 12.3 %reshape.10 = f32[768,32,32]{2,1,0:T(8,128)} reshape(f32[16,49152]{1,0:T(8,128)} %reduce) | data formatting | bytes 6291456
  101.2 14.4 %copy.18 = f32[32,32,16,48]{0,2,3,1:T(8,128)} copy(f32[32,32,16,48]{1,0,3,2:T(8,128)} %bitcast.19) | data formatting | bytes 6291456 | tf_op jit(solution)/shard_map/all_to_all | solution.py:14
  115.5 10.0 all_to_all.16
  125.5 0.0 copy-start.1
  125.5 13.4 %convolution_bitcast_fusion = f32[512,512]{1,0:T(8,128)} fusion(f32[512,32,48]{0,2,1:T(8,128)} %all_to_all.16), kind=kOutput, calls=%fused_computation.2 | convolution fusion | flops 4831838208 | bytes 4194304 | tf_op jit(solution)/shard_map/tps,ups->tu/dot_general | solution.py:16
  138.9 0.0 reduce-scatter.3.cloned.1.call-update
  139.0 0.0 all-reduce.2.cloned.1.call-start
  139.0 77.2 %reduce-scatter.3.cloned.1.call-done = f32[32,512]{1,0:T(8,128)} async-done(((f32[512,512]{1,0:T(8,128)}), f32[32,512]{1,0:T(8,128)}) %reduce-scatter.3.cloned.1.call-update) | async-done | bytes 65552 | tf_op jit(solution)/shard_map/reduce_scatter | solution.py:15
  216.2 0.0 all-reduce.2.cloned.1.call-update
  216.2 0.3 reduce-scatter.5.cloned.1.call-start
  216.5 0.0 copy-done
  216.5 0.0 copy-done.1
  216.5 7.1 fusion
  223.6 6.3 copy.21
  229.9 0.0 reduce-scatter.5.cloned.1.call-update
  229.9 86.9 %all-reduce.2.cloned.1.call-done = f32[32,512]{1,0:T(8,128)} async-done(((f32[32,512]{1,0:T(8,128)}), f32[32,512]{1,0:T(8,128)}) %all-reduce.2.cloned.1.call-update) | async-done | bytes 65552 | tf_op jit(solution)/shard_map/psum | solution.py:21
  316.8 1.5 broadcast_multiply_fusion
  318.3 88.0 %reduce-scatter.5.cloned.1.call-done = f32[4,32,768]{2,1,0:T(8,128)} async-done(((f32[64,32,768]{2,1,0:T(8,128)}), f32[4,32,768]{2,1,0:T(8,128)}) %reduce-scatter.5.cloned.1.call-update) | async-done | bytes 393232 | tf_op jit(solution)/shard_map/reduce_scatter | solution.py:25
  406.2 1.3 copy.22
  407.5 2.4 all_gather.3
  409.9 1.7 convolution_bitcast_fusion.1
  411.6 687.0 %psum.15 = f32[32,64]{1,0:T(8,128)S(1)} all-reduce(f32[32,64]{1,0:T(8,128)S(1)} %convolution_bitcast_fusion.1), channel_id=1, replica_groups=mesh['space'=8,'tm'=16,'param'=2] {'space','tm'}, use_global_device_ids=true, to_apply=%region_3.0 | all-reduce | flops 2048 | bytes 16384 | tf_op jit(solution)/shard_map/psum | solution.py:37
  1098.6 0.6 broadcast_multiply_fusion.1
Async XLA Ops:
  7.2 209.3 %copy-start = (f32[512,64]{0,1:T(8,128)S(1)}, f32[512,64]{0,1:T(8,128)}, u32[]{:S(2)}) copy-start(f32[512,64]{0,1:T(8,128)} %param.3) | copy-start | bytes 393220
  7.2 209.0 %reduce-scatter.3.cloned.1.call-start = ((), (), s32[]{:S(2)}) async-start(), calls=%async_computation.3 | async-start | bytes 1114112 | tf_op jit(solution)/shard_map/reduce_scatter | solution.py:15
  125.5 91.0 %copy-start.1 = (f32[32,32,768]{2,1,0:T(8,128)S(1)}, f32[32,32,768]{2,1,0:T(8,128)}, u32[]{:S(2)}) copy-start(f32[32,32,768]{2,1,0:T(8,128)} %param.2) | copy-start | bytes 9437188
  139.0 177.8 %all-reduce.2.cloned.1.call-start = ((), (), s32[]{:S(2)}) async-start(), calls=%async_computation.4 | async-start | bytes 131072 | tf_op jit(solution)/shard_map/psum | solution.py:21
  216.2 190.0 %reduce-scatter.5.cloned.1.call-start = ((), (), s32[]{:S(2)}) async-start(), calls=%async_computation.5 | async-start | bytes 6684672 | tf_op jit(solution)/shard_map/reduce_scatter | solution.py:25
Sparse Core Ops, SparseCore 0:
  139.1 77.0 reduce-scatter.2
  218.6 98.1 all-reduce.1
  321.1 85.0 reduce-scatter.4
where the time goes:
time: 1110 us
  blocking collectives  734 us (66%)
  waiting for transfers between devices  252 us (23%)
  local copies, waits for them, and re-layouts  70.1 us (6%)
  matrix products  22.3 us (2%)
  between operations  13.8 us (1%)
  other arithmetic  12.9 us (1%)
    psum x1, blocking collectives, body(): lax.psum(param_part, ('space', 'tm')) / (rank_all * total_points)  687 us
    reduce_scatter x1, waiting for transfers between devices, body(): lax.psum_scatter(jnp.einsum('tr,tps->rps', basis_rows, snapshots, precisi...  88 us
    psum x1, waiting for transfers between devices, body(): lax.psum(rows_part, ('space', 'param')) / (all_loads * total_points)  86.9 us
    reduce_scatter x1, waiting for transfers between devices, body(): lax.psum_scatter(jnp.einsum('tps,ups->tu', traded, traded, precision=prec...  77.2 us
    all_to_all x1, blocking collectives, body(): lax.all_to_all(snapshots, 'tm', split_axis=2, concat_axis=0, tiled=True)  44.9 us
    unnamed x7, local copies, waits for them, and re-layouts  37.7 us
    all_to_all x3, local copies, waits for them, and re-layouts, body(): lax.all_to_all(snapshots, 'tm', split_axis=2, concat_axis=0, tiled=True)  24.8 us
  transfers between devices with their start and end apart: 3, of which 3 were waited for; matrix products, arithmetic and copies ran while one was open for 1% of the time, Pallas kernels for 0%

commit v1 on v0

v1 whole, which is shorter than its diff:
```python
import functools

import jax
import jax.numpy as jnp
from jax import lax
from jax.experimental import pallas as pl
from jax.experimental.pallas import tpu as pltpu
from jax.sharding import PartitionSpec as P

MESH = pl.DeviceIdType.MESH
NT = (((1,), (1,)), ((), ()))
NN = (((1,), (0,)), ((), ()))
LANE = 128
ORDER = (
    (1, 0), (0, 1), (3, 0), (0, 3), (1, 1), (3, 3), (1, 3), (3, 1),
    (2, 0), (0, 2), (2, 1), (1, 2), (2, 3), (3, 2), (2, 2),
)


def dot(a, b, dims):
    return lax.dot_general(a, b, dims, preferred_element_type=jnp.float32)


def split(v):
    high = v.astype(jnp.bfloat16)
    return high, (v - high.astype(jnp.float32)).astype(jnp.bfloat16)


def kernel(
    scale_time, scale_param,
    x_hbm, basis_ref, time_out, core_out, param_out,
    staged, sent, held, high_buf, low_buf, basis_high, basis_low,
    gram, gram_sib, gram_sum, gram_rows, tile_in, tile_mine, tiles,
    core_sent, core_held, core_sib, rank_high, rank_low,
    part_mine, part_in, part_sum, part_z,
    load_sem, x_send, x_recv, c_send, c_recv, cs_sem, cs_rsem,
    gs_send, gs_recv, gr_send, gr_recv, gz_send, gz_recv, ga_send, ga_recv,
    px_send, px_recv, pz_send, pz_recv,
):
    sp, tm, me = lax.axis_index("space"), lax.axis_index("tm"), lax.axis_index("param")
    y, x = tm // 4, lax.rem(tm, 4)
    chunks = staged.shape[0]
    steps = staged.shape[1]

    def peer(dx, dy):
        return lax.rem(y + dy, 4) * 4 + lax.rem(x + dx, 4)

    def along(dz):
        return lax.rem(sp + dz, 8)

    def remote(src, dst, ssem, rsem, target):
        return pltpu.make_async_remote_copy(
            src_ref=src, dst_ref=dst, send_sem=ssem, recv_sem=rsem,
            device_id=target, device_id_type=MESH,
        )

    sibling = (sp, tm, 1 - me)

    for k in range(chunks):
        pltpu.make_async_copy(
            x_hbm.at[:, :, pl.ds(k * LANE, LANE)], staged.at[k], load_sem.at[k]
        ).start()

    barrier = pltpu.get_barrier_semaphore()
    for dx, dy in ORDER:
        pl.semaphore_signal(barrier, inc=1, device_id=(sp, peer(dx, dy), me), device_id_type=MESH)
    for dz in range(8):
        if dz:
            pl.semaphore_signal(barrier, inc=1, device_id=(along(dz), tm, me), device_id_type=MESH)
        pl.semaphore_signal(barrier, inc=1, device_id=(along(dz), tm, 1 - me), device_id_type=MESH)

    for k in range(chunks):
        pltpu.make_async_copy(
            x_hbm.at[:, :, pl.ds(k * LANE, LANE)], staged.at[k], load_sem.at[k]
        ).wait()
        flat = staged.at[k].reshape(steps * steps, LANE)
        for j in range(16):
            for pp in range(2):
                sent[k, j, pp] = flat[pl.ds(2 * j + pp, steps, stride=steps), :]
        held[k, tm] = sent[k, tm]
        if k == 0:
            pl.semaphore_wait(barrier, 30)
        for dx, dy in ORDER:
            to = peer(dx, dy)
            remote(
                sent.at[k, to], held.at[k, tm], x_send, x_recv.at[k], (sp, to, me)
            ).start()

    row = lax.broadcasted_iota(jnp.int32, (128, 64), 0)
    col = lax.broadcasted_iota(jnp.int32, (128, 64), 1)
    parts = split(basis_ref[...])
    for pp in range(2):
        pick = jnp.where(
            (lax.rem(row, 8) // 4 == pp) & (col == (row // 8) * 4 + lax.rem(row, 4)), 1.0, 0.0
        ).astype(jnp.bfloat16)
        basis_high[pp] = dot(pick, parts[0], NT).astype(jnp.bfloat16)
        basis_low[pp] = dot(pick, parts[1], NT).astype(jnp.bfloat16)

    gram[...] = jnp.zeros_like(gram)

    for k in range(chunks):
        remote(
            sent.at[k, pl.ds(0, 15)], held.at[k, pl.ds(0, 15)], x_send, x_recv.at[k], sibling
        ).wait_recv()
        for pp in range(2):
            high, low = split(held[k, :, pp].reshape(512, LANE))
            high_buf[:, pp * LANE:(pp + 1) * LANE] = high
            low_buf[:, pp * LANE:(pp + 1) * LANE] = low
        total = None
        for pp in range(2):
            high = high_buf[:, pp * LANE:(pp + 1) * LANE]
            low = low_buf[:, pp * LANE:(pp + 1) * LANE]
            term = (
                dot(basis_high[pp], low, NN) + dot(basis_low[pp], high, NN)
            ) + dot(basis_high[pp], high, NN)
            total = term if total is None else total + term
        core_sent[k] = total.reshape(16, 8, LANE)
        core_held[k, tm] = core_sent[k, tm]
        for dx, dy in ORDER:
            to = peer(dx, dy)
            remote(
                core_sent.at[k, to], core_held.at[k, tm], c_send, c_recv, (sp, to, me)
            ).start()
        for dy in range(4):
            there = lax.rem(y + dy, 4)
            rows = pl.ds(pl.multiple_of(there * 128, 128), 128)
            high, low = high_buf[rows, :], low_buf[rows, :]
            add = (
                dot(high, low_buf[...], NT) + dot(low, high_buf[...], NT)
            ) + dot(high, high_buf[...], NT)
            blocks = pl.ds(there * 4, 4)
            gram[blocks] = gram[blocks] + add.reshape(4, 2, 16, 512)
            if k == chunks - 1:
                remote(
                    gram.at[blocks, 1 - me], gram_sib.at[blocks],
                    gs_send.at[dy], gs_recv.at[dy], sibling,
                ).start()

    for dy in range(4):
        blocks = pl.ds(lax.rem(y + dy, 4) * 4, 4)
        remote(
            gram.at[blocks, 1 - me], gram_sib.at[blocks],
            gs_send.at[dy], gs_recv.at[dy], sibling,
        ).wait_recv()
        gram_sum[blocks] = gram[blocks, me] + gram_sib[blocks]
        for dx in range(4):
            to = peer(dx, dy)
            if dx == 0 and dy == 0:
                gram_rows[tm] = gram_sum[tm]
            else:
                remote(
                    gram_sum.at[to], gram_rows.at[tm], gr_send, gr_recv, (sp, to, me)
                ).start()

    remote(
        sent.at[0, pl.ds(0, 15)], core_held.at[:, pl.ds(0, 15)], c_send, c_recv, sibling
    ).wait_recv()
    swap = remote(core_held, core_sib, cs_sem, cs_rsem, sibling)
    swap.start()
    for k in range(chunks):
        flat = core_held.at[k].reshape(128, LANE)
        for r in range(4):
            v = flat[pl.ds(r, 32, stride=4), :]
            core_out[r, :, k * LANE:(k + 1) * LANE] = v
            high, low = split(v)
            rank_high[me, r, :, k * LANE:(k + 1) * LANE] = high
            rank_low[me, r, :, k * LANE:(k + 1) * LANE] = low
    swap.wait_recv()
    for k in range(chunks):
        flat = core_sib.at[k].reshape(128, LANE)
        for r in range(4):
            high, low = split(flat[pl.ds(r, 32, stride=4), :])
            rank_high[1 - me, r, :, k * LANE:(k + 1) * LANE] = high
            rank_low[1 - me, r, :, k * LANE:(k + 1) * LANE] = low
    part = jnp.zeros((32, 64), jnp.float32)
    for r in range(4):
        high, low = rank_high[me, r], rank_low[me, r]
        all_high = rank_high[:, r].reshape(64, high.shape[1])
        all_low = rank_low[:, r].reshape(64, high.shape[1])
        part = part + (
            (dot(high, all_low, NT) + dot(low, all_high, NT)) + dot(high, all_high, NT)
        )
    part_mine[...] = jnp.concatenate([part[:16], part[16:]], axis=1)
    part_in[tm] = part_mine[...]
    for dx, dy in ORDER:
        remote(
            part_mine, part_in.at[tm], px_send, px_recv, (sp, peer(dx, dy), me)
        ).start()

    remote(
        gram_sum.at[pl.ds(0, 15)], gram_rows.at[pl.ds(0, 15)], gr_send, gr_recv, sibling
    ).wait_recv()
    rows = gram_rows[0]
    for j in range(1, 16):
        rows = rows + gram_rows[j]
    for q in range(8):
        tile_mine[q] = rows[(q // 4) * 8:(q // 4) * 8 + 8, (q % 4) * LANE:(q % 4 + 1) * LANE]
    tile_in[sp] = tile_mine[sp]
    for dz in (1, 7, 2, 6, 3, 5, 4):
        to = along(dz)
        remote(tile_mine.at[to], tile_in.at[sp], gz_send, gz_recv, (to, tm, me)).start()

    remote(
        part_in.at[pl.ds(0, 15)], part_in.at[pl.ds(0, 15)], px_send, px_recv, sibling
    ).wait_recv()
    part = part_in[0]
    for j in range(1, 16):
        part = part + part_in[j]
    part_sum[...] = part
    part_z[sp] = part
    for dz in (1, 7, 2, 6, 3, 5, 4):
        to = along(dz)
        remote(part_sum, part_z.at[sp], pz_send, pz_recv, (to, tm, me)).start()

    remote(
        tile_mine.at[pl.ds(0, 7)], tile_in.at[pl.ds(0, 7)], gz_send, gz_recv, sibling
    ).wait_recv()
    tile = tile_in[0]
    for j in range(1, 8):
        tile = tile + tile_in[j]
    slot = me * 8 + sp
    tiles[slot] = tile * scale_time
    for dz in (0, 1, 7, 2, 6, 3, 5, 4):
        to = along(dz)
        if dz:
            remote(tiles.at[slot], tiles.at[slot], ga_send, ga_recv, (to, tm, me)).start()
        remote(tiles.at[slot], tiles.at[slot], ga_send, ga_recv, (to, tm, 1 - me)).start()

    remote(
        part_z.at[pl.ds(0, 7)], part_z.at[pl.ds(0, 7)], pz_send, pz_recv, sibling
    ).wait_recv()
    part = part_z[0]
    for j in range(1, 8):
        part = part + part_z[j]
    part = part * scale_param
    param_out[0:16, :] = part[:, :64]
    param_out[16:32, :] = part[:, 64:]

    remote(
        tiles.at[pl.ds(0, 15)], tiles.at[pl.ds(0, 15)], ga_send, ga_recv, sibling
    ).wait_recv()
    for q in range(16):
        time_out[(q // 4) * 8:(q // 4) * 8 + 8, (q % 4) * LANE:(q % 4 + 1) * LANE] = tiles[q]

    remote(
        sent.at[:, pl.ds(0, 15)], held.at[:, pl.ds(0, 15)], x_send, x_recv.at[0], sibling
    ).wait_send()
    remote(
        core_sent.at[:, pl.ds(0, 15)], core_held.at[:, pl.ds(0, 15)], c_send, c_recv, sibling
    ).wait_send()
    for dy in range(4):
        blocks = pl.ds(lax.rem(y + dy, 4) * 4, 4)
        remote(
            gram.at[blocks, 1 - me], gram_sib.at[blocks],
            gs_send.at[dy], gs_recv.at[dy], sibling,
        ).wait_send()
    swap.wait_send()
    remote(
        gram_sum.at[pl.ds(0, 15)], gram_rows.at[pl.ds(0, 15)], gr_send, gr_recv, sibling
    ).wait_send()
    remote(
        part_in.at[pl.ds(0, 15)], part_in.at[pl.ds(0, 15)], px_send, px_recv, sibling
    ).wait_send()
    remote(
        tile_mine.at[pl.ds(0, 7)], tile_in.at[pl.ds(0, 7)], gz_send, gz_recv, sibling
    ).wait_send()
    remote(
        part_z.at[pl.ds(0, 7)], part_z.at[pl.ds(0, 7)], pz_send, pz_recv, sibling
    ).wait_send()
    remote(
        tiles.at[pl.ds(0, 15)], tiles.at[pl.ds(0, 15)], ga_send, ga_recv, sibling
    ).wait_send()


def body(snapshots, time_basis):
    f32, bf16 = jnp.float32, jnp.bfloat16
    time_local, load_local, point_local = snapshots.shape
    columns = load_local * 2 * point_local * 8
    rank = time_basis.shape[1]
    k = point_local // LANE
    vmem = pltpu.VMEM
    dma = pltpu.SemaphoreType.DMA
    return pl.pallas_call(
        functools.partial(kernel, 1.0 / columns, 1.0 / (rank * point_local * 8)),
        out_shape=(
            jax.ShapeDtypeStruct((32, 512), f32),
            jax.ShapeDtypeStruct((4, 32, point_local), f32),
            jax.ShapeDtypeStruct((32, 64), f32),
        ),
        in_specs=[pl.BlockSpec(memory_space=pl.ANY), pl.BlockSpec(memory_space=vmem)],
        out_specs=(pl.BlockSpec(memory_space=vmem),) * 3,
        scratch_shapes=[
            vmem((k, time_local, load_local, LANE), f32),
            vmem((k, 16, 2, time_local, LANE), f32),
            vmem((k, 16, 2, time_local, LANE), f32),
            vmem((512, 2 * LANE), bf16),
            vmem((512, 2 * LANE), bf16),
            vmem((2, 128, 512), bf16),
            vmem((2, 128, 512), bf16),
            vmem((16, 2, 16, 512), f32),
            vmem((16, 16, 512), f32),
            vmem((16, 16, 512), f32),
            vmem((16, 16, 512), f32),
            vmem((8, 8, LANE), f32),
            vmem((8, 8, LANE), f32),
            vmem((16, 8, LANE), f32),
            vmem((k, 16, 8, LANE), f32),
            vmem((k, 16, 8, LANE), f32),
            vmem((k, 16, 8, LANE), f32),
            vmem((2, 4, 32, point_local), bf16),
            vmem((2, 4, 32, point_local), bf16),
            vmem((16, LANE), f32),
            vmem((16, 16, LANE), f32),
            vmem((16, LANE), f32),
            vmem((8, 16, LANE), f32),
            dma((k,)), dma, dma((k,)), dma, dma, dma, dma,
            dma((4,)), dma((4,)), dma, dma, dma, dma, dma, dma,
            dma, dma, dma, dma,
        ],
        compiler_params=pltpu.CompilerParams(
            collective_id=0, has_side_effects=True, vmem_limit_bytes=56 * 1024 * 1024
        ),
    )(snapshots, time_basis)


def solution(mesh):
    return jax.shard_map(
        body,
        mesh=mesh,
        in_specs=(P("tm", "param", "space"), P()),
        out_specs=(P("tm", None), P("tm", "param", "space"), P("param", None)),
        check_vma=False,
    )
```

time: 1110 us -> 79.6 us (0.07)
  the two profiles are of different devices: /device:TPU:0 before, /device:TPU:1 now
where the time goes in v1:
time: 79.6 us; the launch traced here: 79.3 us
  Pallas kernels  72.3 us (91%)
  local copies, waits for them, and re-layouts  6.31 us (8%)
    pallas_call x1, Pallas kernels, body(): pl.pallas_call(functools.partial(kernel, 1.0 / columns, 1.0 / (rank * poi...  72.3 us
    unnamed x4, local copies, waits for them, and re-layouts  6.31 us

profile of v1, /device:TPU:1, one launch (start us, length us, event | category | flops | bytes accessed | tf_op | source)
XLA Modules:
  0.0 79.3 jit_solution(17942115290221277475)
XLA Ops:
  0.6 1.7 %copy.5.basis_ref = f32[512,64]{1,0:T(8,128)} copy(f32[512,64]{0,1:T(8,128)} %param.3) | data formatting | bytes 262144 | tf_op args[1]
  2.4 72.3 %shard_map.49 = (f32[32,512]{1,0:T(8,128)}, f32[4,32,768]{2,1,0:T(8,128)}, f32[32,64]{1,0:T(8,128)}) custom-call(f32[32,32,768]{2,1,0:T(8,128)} %x_hbm.1, f32[512,64]{1,0:T(8,128)} %copy.5.basis_ref), custom_call_target="tpu_custom_call" | custom-call | tf_op jit(solution)/shard_map/pallas_call | solution.py:283
  74.7 1.5 %copy.9 = f32[32,512]{1,0:T(8,128)} copy(f32[32,512]{1,0:T(8,128)} %get-tuple-element.6) | data formatting | bytes 131072
  76.2 1.8 %copy.10 = f32[4,32,768]{2,1,0:T(8,128)} copy(f32[4,32,768]{2,1,0:T(8,128)} %get-tuple-element.7) | data formatting | bytes 786432
  78.0 1.3 %copy.11 = f32[32,64]{1,0:T(8,128)} copy(f32[32,64]{1,0:T(8,128)} %get-tuple-element.8) | data formatting | bytes 16384

commit v2 on v1

v2 whole, which is shorter than its diff:
```python
import functools

import jax
import jax.numpy as jnp
from jax import lax
from jax.experimental import pallas as pl
from jax.experimental.pallas import tpu as pltpu
from jax.sharding import PartitionSpec as P

MESH = pl.DeviceIdType.MESH
NT = (((1,), (1,)), ((), ()))
NN = (((1,), (0,)), ((), ()))
LANE = 128
ORDER = (
    (1, 0), (0, 1), (3, 0), (0, 3), (1, 1), (3, 3), (1, 3), (3, 1),
    (2, 0), (0, 2), (2, 1), (1, 2), (2, 3), (3, 2), (2, 2),
)


def dot(a, b, dims):
    return lax.dot_general(a, b, dims, preferred_element_type=jnp.float32)


def split(v):
    high = v.astype(jnp.bfloat16)
    return high, (v - high.astype(jnp.float32)).astype(jnp.bfloat16)


def split_3(v):
    high = v.astype(jnp.bfloat16)
    rest = v - high.astype(jnp.float32)
    return (high,) + split(rest)


def kernel(
    scale_time, scale_param,
    x_hbm, basis_ref, time_out, core_out, param_out,
    staged, sent, mid, held, high_buf, low_buf, basis_high, basis_low,
    gram, gram_sib, gram_sum, gram_in, rows_mine, rows_in, tiles,
    core_sent, core_held, core_sib, pair_gram, pair_kept,
    part_mine, part_in, part_sum, part_z,
    load_sem, x1_send, x1_recv, x2_send, x2_recv, c_send, c_recv, cs_send, cs_recv,
    gs_send, gs_recv, g1_send, g1_recv, gz_send, gz_recv, gy_send, gy_recv,
    px_send, px_recv, pz_send, pz_recv,
):
    sp, tm, me = lax.axis_index("space"), lax.axis_index("tm"), lax.axis_index("param")
    y, x = tm // 4, lax.rem(tm, 4)
    chunks, steps = staged.shape[0], staged.shape[1]

    def peer(dx, dy):
        return lax.rem(y + dy, 4) * 4 + lax.rem(x + dx, 4)

    def along(dz):
        return lax.rem(sp + dz, 8)

    def remote(src, dst, ssem, rsem, target):
        return pltpu.make_async_remote_copy(
            src_ref=src, dst_ref=dst, send_sem=ssem, recv_sem=rsem,
            device_id=target, device_id_type=MESH,
        )

    sibling = (sp, tm, 1 - me)
    ring = (1, 3, 2)
    far = (4, 3, 5, 2, 6, 1, 7)

    def load(k):
        return pltpu.make_async_copy(
            x_hbm.at[:, :, pl.ds(k * LANE, LANE)], staged.at[k], load_sem.at[k]
        )

    for k in range(chunks):
        load(k).start()

    barrier = pltpu.get_barrier_semaphore()
    for dz in far:
        pl.semaphore_signal(barrier, inc=1, device_id=(along(dz), tm, me), device_id_type=MESH)
    for dx, dy in ORDER[::-1]:
        pl.semaphore_signal(barrier, inc=1, device_id=(sp, peer(dx, dy), me), device_id_type=MESH)
    pl.semaphore_signal(barrier, inc=1, device_id=sibling, device_id_type=MESH)

    for k in range(chunks):
        load(k).wait()
        flat = staged.at[k].reshape(steps * steps, LANE)
        for j in range(16):
            for pp in range(2):
                sent[k, pp, j // 4, j % 4] = flat[pl.ds(2 * j + pp, steps, stride=steps), :]
        if k == 0:
            pl.semaphore_wait(barrier, 23)
        for d in ring:
            tx, ty = lax.rem(x + d, 4), lax.rem(y + d, 4)
            remote(
                sent.at[k, 0, :, tx], mid.at[k, 0, x], x1_send, x1_recv.at[k, 0],
                (sp, y * 4 + tx, me),
            ).start()
            remote(
                sent.at[k, 1, ty], mid.at[k, 1, y], x1_send, x1_recv.at[k, 1],
                (sp, ty * 4 + x, me),
            ).start()
        mid[k, 0, x] = sent[k, 0, :, x]
        mid[k, 1, y] = sent[k, 1, y]

    row = lax.broadcasted_iota(jnp.int32, (128, 64), 0)
    col = lax.broadcasted_iota(jnp.int32, (128, 64), 1)
    parts = split(basis_ref[...])
    for pp in range(2):
        pick = jnp.where(
            (lax.rem(row, 8) // 4 == pp) & (col == (row // 8) * 4 + lax.rem(row, 4)), 1.0, 0.0
        ).astype(jnp.bfloat16)
        basis_high[pp] = dot(pick, parts[0], NN).astype(jnp.bfloat16)
        basis_low[pp] = dot(pick, parts[1], NN).astype(jnp.bfloat16)

    gram[...] = jnp.zeros_like(gram)
    pair_gram[...] = jnp.zeros_like(pair_gram)

    for k in range(chunks):
        for pp in range(2):
            remote(
                sent.at[k, pp, pl.ds(0, 3)], mid.at[k, pp, pl.ds(0, 3)],
                x1_send, x1_recv.at[k, pp], sibling,
            ).wait_recv()
        for d in ring:
            tx, ty = lax.rem(x + d, 4), lax.rem(y + d, 4)
            remote(
                mid.at[k, 0, :, ty], held.at[k, 0, y], x2_send, x2_recv.at[k],
                (sp, ty * 4 + x, me),
            ).start()
            remote(
                mid.at[k, 1, :, tx], held.at[k, 1, :, x], x2_send, x2_recv.at[k],
                (sp, y * 4 + tx, me),
            ).start()
        held[k, 0, y] = mid[k, 0, :, y]
        held[k, 1, :, x] = mid[k, 1, :, x]

    def core_back(k):
        remote(
            core_sent.at[k, pl.ds(0, 15)], core_held.at[k, pl.ds(0, 15)],
            c_send, c_recv.at[k], sibling,
        ).wait_recv()
        remote(
            core_held.at[k], core_sib.at[k], cs_send.at[k], cs_recv.at[k], sibling
        ).start()

    def core_write(k):
        flat = core_held.at[k].reshape(128, LANE)
        for r in range(4):
            core_out[r, :, k * LANE:(k + 1) * LANE] = flat[pl.ds(r, 32, stride=4), :]

    def core_pair(k):
        remote(
            core_held.at[k], core_sib.at[k], cs_send.at[k], cs_recv.at[k], sibling
        ).wait_recv()
        high, low = split(core_held[k].reshape(128, LANE))
        high_2, low_2 = split(core_sib[k].reshape(128, LANE))
        pair_gram[0] += (dot(high, low, NT) + dot(low, high, NT)) + dot(high, high, NT)
        pair_gram[1] += (dot(high, low_2, NT) + dot(low, high_2, NT)) + dot(high, high_2, NT)

    for k in range(chunks):
        remote(
            mid.at[k, :, pl.ds(0, 3)], held.at[k, :, pl.ds(0, 3)],
            x2_send, x2_recv.at[k], sibling,
        ).wait_recv()
        for pp in range(2):
            high, low = split(held[k, pp].reshape(512, LANE))
            high_buf[:, pp * LANE:(pp + 1) * LANE] = high
            low_buf[:, pp * LANE:(pp + 1) * LANE] = low
        total = None
        for pp in range(2):
            high = high_buf[:, pp * LANE:(pp + 1) * LANE]
            low = low_buf[:, pp * LANE:(pp + 1) * LANE]
            term = (
                dot(basis_high[pp], low, NN) + dot(basis_low[pp], high, NN)
            ) + dot(basis_high[pp], high, NN)
            total = term if total is None else total + term
        core_sent[k] = total.reshape(16, 8, LANE)
        core_held[k, tm] = core_sent[k, tm]
        for dx, dy in ORDER:
            to = peer(dx, dy)
            remote(
                core_sent.at[k, to], core_held.at[k, tm], c_send, c_recv.at[k], (sp, to, me)
            ).start()
        for dy in range(4):
            there = lax.rem(y + dy, 4)
            rows = pl.ds(pl.multiple_of(there * 128, 128), 128)
            high, low = high_buf[rows, :], low_buf[rows, :]
            add = (
                dot(high, low_buf[...], NT) + dot(low, high_buf[...], NT)
            ) + dot(high, high_buf[...], NT)
            blocks = pl.ds(there * 4, 4)
            gram[blocks] = gram[blocks] + add.reshape(4, 2, 16, 512)
            if k == chunks - 1:
                remote(
                    gram.at[blocks, 1 - me], gram_sib.at[blocks],
                    gs_send.at[dy], gs_recv.at[dy], sibling,
                ).start()

    for dy in range(4):
        there = lax.rem(y + dy, 4)
        blocks = pl.ds(there * 4, 4)
        remote(
            gram.at[blocks, 1 - me], gram_sib.at[blocks],
            gs_send.at[dy], gs_recv.at[dy], sibling,
        ).wait_recv()
        gram_sum[blocks] = gram[blocks, me] + gram_sib[blocks]
        for dx in (1, 3, 2, 0):
            to = peer(dx, dy)
            if dx or dy:
                remote(
                    gram_sum.at[to], gram_in.at[tm], g1_send, g1_recv, (sp, to, me)
                ).start()
    gram_in[tm] = gram_sum[tm]

    for k in range(chunks):
        core_back(k)
    for k in range(chunks):
        core_pair(k)
    row = lax.broadcasted_iota(jnp.int32, (128, 128), 0)
    col = lax.broadcasted_iota(jnp.int32, (128, 128), 1)
    same = lax.rem(row, 4) == lax.rem(col, 4)
    row = lax.broadcasted_iota(jnp.int32, (64, 128), 0)
    col = lax.broadcasted_iota(jnp.int32, (64, 128), 1)
    part = jnp.zeros((32, 64), jnp.float32)
    for other in range(2):
        at = (1 - me) if other else me
        place = jnp.where(row == at * 32 + col // 4, 1.0, 0.0).astype(jnp.bfloat16)
        pair_kept[...] = jnp.where(same, pair_gram[other], 0.0)
        summed = (
            (pair_kept[pl.ds(0, 32, stride=4), :] + pair_kept[pl.ds(1, 32, stride=4), :])
            + (pair_kept[pl.ds(2, 32, stride=4), :] + pair_kept[pl.ds(3, 32, stride=4), :])
        )
        for small in split_3(summed):
            part = part + dot(small, place, NT)
    part_mine[...] = jnp.concatenate([part[:16], part[16:]], axis=1)
    for dx, dy in ORDER[::-1]:
        remote(
            part_mine, part_in.at[tm], px_send, px_recv, (sp, peer(dx, dy), me)
        ).start()
    part_in[tm] = part_mine[...]

    remote(
        gram_sum.at[pl.ds(0, 15)], gram_in.at[pl.ds(0, 15)], g1_send, g1_recv, sibling
    ).wait_recv()
    rows = gram_in[0]
    for j in range(1, 16):
        rows = rows + gram_in[j]
    rows_mine[...] = rows
    for dz in far:
        remote(
            rows_mine, rows_in.at[sp], gz_send, gz_recv, (along(dz), tm, me)
        ).start()
    rows_in[sp] = rows

    remote(
        part_in.at[pl.ds(0, 15)], part_in.at[pl.ds(0, 15)], px_send, px_recv, sibling
    ).wait_recv()
    part = part_in[0]
    for j in range(1, 16):
        part = part + part_in[j]
    part_sum[...] = part
    for dz in far:
        to = along(dz)
        remote(part_sum, part_z.at[sp], pz_send, pz_recv, (to, tm, me)).start()
    part_z[sp] = part

    for k in range(chunks):
        core_write(k)

    remote(
        gram_in.at[pl.ds(0, 7)], rows_in.at[pl.ds(0, 7)], gz_send, gz_recv, sibling
    ).wait_recv()
    rows = rows_in[0]
    for j in range(1, 8):
        rows = rows + rows_in[j]
    tiles[me] = rows * scale_time
    swap = remote(tiles.at[me], tiles.at[me], gy_send, gy_recv, sibling)
    swap.start()

    remote(
        part_z.at[pl.ds(0, 7)], part_z.at[pl.ds(0, 7)], pz_send, pz_recv, sibling
    ).wait_recv()
    part = part_z[0]
    for j in range(1, 8):
        part = part + part_z[j]
    part = part * scale_param
    param_out[0:16, :] = part[:, :64]
    param_out[16:32, :] = part[:, 64:]

    swap.wait_recv()
    time_out[0:16, :] = tiles[0]
    time_out[16:32, :] = tiles[1]

    remote(
        sent.at[:, :, pl.ds(0, 3)], mid.at[:, :, pl.ds(0, 3)], x1_send, x1_recv.at[0, 0], sibling
    ).wait_send()
    remote(
        mid.at[:, :, pl.ds(0, 3)], held.at[:, :, pl.ds(0, 3)], x2_send, x2_recv.at[0], sibling
    ).wait_send()
    remote(
        core_sent.at[:, pl.ds(0, 15)], core_held.at[:, pl.ds(0, 15)],
        c_send, c_recv.at[0], sibling,
    ).wait_send()
    for k in range(chunks):
        remote(
            core_held.at[k], core_sib.at[k], cs_send.at[k], cs_recv.at[k], sibling
        ).wait_send()
    for dy in range(4):
        blocks = pl.ds(lax.rem(y + dy, 4) * 4, 4)
        remote(
            gram.at[blocks, 1 - me], gram_sib.at[blocks],
            gs_send.at[dy], gs_recv.at[dy], sibling,
        ).wait_send()
    remote(
        gram_sum.at[pl.ds(0, 15)], gram_in.at[pl.ds(0, 15)], g1_send, g1_recv, sibling
    ).wait_send()
    remote(
        gram_in.at[pl.ds(0, 7)], rows_in.at[pl.ds(0, 7)], gz_send, gz_recv, sibling
    ).wait_send()
    swap.wait_send()
    remote(
        part_in.at[pl.ds(0, 15)], part_in.at[pl.ds(0, 15)], px_send, px_recv, sibling
    ).wait_send()
    remote(
        part_z.at[pl.ds(0, 7)], part_z.at[pl.ds(0, 7)], pz_send, pz_recv, sibling
    ).wait_send()


def body(snapshots, time_basis):
    f32, bf16 = jnp.float32, jnp.bfloat16
    time_local, load_local, point_local = snapshots.shape
    columns = load_local * 2 * point_local * 8
    rank = time_basis.shape[1]
    k = point_local // LANE
    vmem = pltpu.VMEM
    dma = pltpu.SemaphoreType.DMA
    block = (k, 2, 4, 4, time_local, LANE)
    return pl.pallas_call(
        functools.partial(kernel, 1.0 / columns, 1.0 / (rank * point_local * 8)),
        out_shape=(
            jax.ShapeDtypeStruct((32, 512), f32),
            jax.ShapeDtypeStruct((4, 32, point_local), f32),
            jax.ShapeDtypeStruct((32, 64), f32),
        ),
        in_specs=[pl.BlockSpec(memory_space=pl.ANY), pl.BlockSpec(memory_space=vmem)],
        out_specs=(pl.BlockSpec(memory_space=vmem),) * 3,
        scratch_shapes=[
            vmem((k, time_local, load_local, LANE), f32),
            vmem(block, f32),
            vmem(block, f32),
            vmem(block, f32),
            vmem((512, 2 * LANE), bf16),
            vmem((512, 2 * LANE), bf16),
            vmem((2, 128, 512), bf16),
            vmem((2, 128, 512), bf16),
            vmem((16, 2, 16, 512), f32),
            vmem((16, 16, 512), f32),
            vmem((16, 16, 512), f32),
            vmem((16, 16, 512), f32),
            vmem((16, 512), f32),
            vmem((8, 16, 512), f32),
            vmem((2, 16, 512), f32),
            vmem((k, 16, 8, LANE), f32),
            vmem((k, 16, 8, LANE), f32),
            vmem((k, 16, 8, LANE), f32),
            vmem((2, 128, 128), f32),
            vmem((128, 128), f32),
            vmem((16, LANE), f32),
            vmem((16, 16, LANE), f32),
            vmem((16, LANE), f32),
            vmem((8, 16, LANE), f32),
            dma((k,)), dma, dma((k, 2)), dma, dma((k,)), dma, dma((k,)), dma((k,)), dma((k,)),
            dma((4,)), dma((4,)), dma, dma, dma, dma, dma, dma,
            dma, dma, dma, dma,
        ],
        compiler_params=pltpu.CompilerParams(
            collective_id=0, has_side_effects=True, vmem_limit_bytes=48 * 1024 * 1024
        ),
    )(snapshots, time_basis.T)


def solution(mesh):
    return jax.shard_map(
        body,
        mesh=mesh,
        in_specs=(P("tm", "param", "space"), P()),
        out_specs=(P("tm", None), P("tm", "param", "space"), P("param", None)),
        check_vma=False,
    )
```

time: 79.6 us -> 75.6 us (0.950)
  Pallas kernels: 72.3 us -> 70.1 us
  local copies, waits for them, and re-layouts: 6.31 us -> 4.77 us
    pallas_call x1, Pallas kernels: 72.3 us -> 70.1 us  [body(): pl.pallas_call(functools.partial(kernel, 1.0 / columns, 1.0 / (rank * poi...]
    unnamed x4 -> x7, local copies, waits for them, and re-layouts: 6.31 us -> 4.77 us
where the time goes in v2:
time: 75.6 us; the launch traced here: 75.5 us
  Pallas kernels  70.1 us (93%)
  local copies, waits for them, and re-layouts  4.77 us (6%)
    pallas_call x1, Pallas kernels, body(): pl.pallas_call(functools.partial(kernel, 1.0 / columns, 1.0 / (rank * poi...  70.1 us
    unnamed x7, local copies, waits for them, and re-layouts  4.77 us

profile of v2, /device:TPU:1, one launch (start us, length us, event | category | flops | bytes accessed | tf_op | source)
XLA Modules:
  0.0 75.5 jit_solution(6075524974708672800)
XLA Ops:
  0.6 0.0 copy-start
  0.6 1.9 %copy-done = f32[32,32,768]{2,1,0:T(8,128)S(1)} copy-done((f32[32,32,768]{2,1,0:T(8,128)S(1)}, f32[32,32,768]{2,1,0:T(8,128)}, u32[]{:S(2)}) %copy-start) | copy-done | bytes 3145752
  2.5 0.0 copy-start.1
  2.5 0.9 %copy-done.1 = f32[512,64]{0,1:T(8,128)S(1)} copy-done((f32[512,64]{0,1:T(8,128)S(1)}, f32[512,64]{0,1:T(8,128)}, u32[]{:S(2)}) %copy-start.1) | copy-done | bytes 131096
  3.4 70.1 %shard_map.49 = (f32[32,512]{1,0:T(8,128)S(1)}, f32[4,32,768]{2,1,0:T(8,128)S(1)}, f32[32,64]{1,0:T(8,128)S(1)}) custom-call(f32[32,32,768]{2,1,0:T(8,128)S(1)} %copy-done, f32[64,512]{1,0:T(8,128)S(1)} %bitcast.1), custom_call_target="tpu_custom_call" | custom-call | tf_op jit(solution)/shard_map/pallas_call | solution.py:335
  73.5 0.6 copy.8
  74.2 0.7 copy.9
  74.9 0.6 copy.10
Async XLA Ops:
  0.6 1.9 %copy-start = (f32[32,32,768]{2,1,0:T(8,128)S(1)}, f32[32,32,768]{2,1,0:T(8,128)}, u32[]{:S(2)}) copy-start(f32[32,32,768]{2,1,0:T(8,128)} %x_hbm.1) | copy-start | bytes 9437188
  2.5 0.9 %copy-start.1 = (f32[512,64]{0,1:T(8,128)S(1)}, f32[512,64]{0,1:T(8,128)}, u32[]{:S(2)}) copy-start(f32[512,64]{0,1:T(8,128)} %param.3) | copy-start | bytes 393220

commit v3 on v2

--- a/solution.py
+++ b/solution.py
@@ -34,12 +34,12 @@
 
 def kernel(
     scale_time, scale_param,
-    x_hbm, basis_ref, time_out, core_out, param_out,
-    staged, sent, mid, held, high_buf, low_buf, basis_high, basis_low,
+    x_hbm, basis_hbm, time_out, core_out, param_out,
+    basis_ref, staged, sent, mid, held, high_buf, low_buf, basis_high, basis_low,
     gram, gram_sib, gram_sum, gram_in, rows_mine, rows_in, tiles,
     core_sent, core_held, core_sib, pair_gram, pair_kept,
     part_mine, part_in, part_sum, part_z,
-    load_sem, x1_send, x1_recv, x2_send, x2_recv, c_send, c_recv, cs_send, cs_recv,
+    relay, basis_sem, load_sem, x1_send, x1_recv, x2_send, x2_recv, c_send, c_recv, cs_send, cs_recv,
     gs_send, gs_recv, g1_send, g1_recv, gz_send, gz_recv, gy_send, gy_recv,
     px_send, px_recv, pz_send, pz_recv,
 ):
@@ -68,15 +68,18 @@
             x_hbm.at[:, :, pl.ds(k * LANE, LANE)], staged.at[k], load_sem.at[k]
         )
 
+    barrier = pltpu.get_barrier_semaphore()
+    for d in (2, 1, 3):
+        pl.semaphore_signal(barrier, inc=1, device_id=(sp, peer(d, 0), me), device_id_type=MESH)
+        pl.semaphore_signal(barrier, inc=1, device_id=(sp, peer(0, d), me), device_id_type=MESH)
+    for dz in (1, 7):
+        pl.semaphore_signal(barrier, inc=1, device_id=(along(dz), tm, me), device_id_type=MESH)
+    pl.semaphore_signal(barrier, inc=1, device_id=sibling, device_id_type=MESH)
+
     for k in range(chunks):
         load(k).start()
-
-    barrier = pltpu.get_barrier_semaphore()
-    for dz in far:
-        pl.semaphore_signal(barrier, inc=1, device_id=(along(dz), tm, me), device_id_type=MESH)
-    for dx, dy in ORDER[::-1]:
-        pl.semaphore_signal(barrier, inc=1, device_id=(sp, peer(dx, dy), me), device_id_type=MESH)
-    pl.semaphore_signal(barrier, inc=1, device_id=sibling, device_id_type=MESH)
+    basis_load = pltpu.make_async_copy(basis_hbm, basis_ref, basis_sem)
+    basis_load.start()
 
     for k in range(chunks):
         load(k).wait()
@@ -85,7 +88,7 @@
             for pp in range(2):
                 sent[k, pp, j // 4, j % 4] = flat[pl.ds(2 * j + pp, steps, stride=steps), :]
         if k == 0:
-            pl.semaphore_wait(barrier, 23)
+            pl.semaphore_wait(barrier, 9)
         for d in ring:
             tx, ty = lax.rem(x + d, 4), lax.rem(y + d, 4)
             remote(
@@ -99,8 +102,15 @@
         mid[k, 0, x] = sent[k, 0, :, x]
         mid[k, 1, y] = sent[k, 1, y]
 
+    def pass_on(n):
+        for dz in (1, 7):
+            pl.semaphore_signal(
+                relay.at[n], inc=1, device_id=(along(dz), tm, me), device_id_type=MESH
+            )
+
     row = lax.broadcasted_iota(jnp.int32, (128, 64), 0)
     col = lax.broadcasted_iota(jnp.int32, (128, 64), 1)
+    basis_load.wait()
     parts = split(basis_ref[...])
     for pp in range(2):
         pick = jnp.where(
@@ -172,6 +182,10 @@
             ) + dot(basis_high[pp], high, NN)
             total = term if total is None else total + term
         core_sent[k] = total.reshape(16, 8, LANE)
+        if 1 <= k <= 3:
+            pl.semaphore_wait(relay.at[k - 1], 2)
+        if k <= 2:
+            pass_on(k)
         core_held[k, tm] = core_sent[k, tm]
         for dx, dy in ORDER:
             to = peer(dx, dy)
@@ -339,9 +353,10 @@
             jax.ShapeDtypeStruct((4, 32, point_local), f32),
             jax.ShapeDtypeStruct((32, 64), f32),
         ),
-        in_specs=[pl.BlockSpec(memory_space=pl.ANY), pl.BlockSpec(memory_space=vmem)],
+        in_specs=[pl.BlockSpec(memory_space=pl.ANY)] * 2,
         out_specs=(pl.BlockSpec(memory_space=vmem),) * 3,
         scratch_shapes=[
+            vmem((rank, 512), f32),
             vmem((k, time_local, load_local, LANE), f32),
             vmem(block, f32),
             vmem(block, f32),
@@ -366,14 +381,18 @@
             vmem((16, 16, LANE), f32),
             vmem((16, LANE), f32),
             vmem((8, 16, LANE), f32),
-            dma((k,)), dma, dma((k, 2)), dma, dma((k,)), dma, dma((k,)), dma((k,)), dma((k,)),
+            pltpu.SemaphoreType.REGULAR((3,)),
+            dma, dma((k,)), dma, dma((k, 2)), dma, dma((k,)), dma, dma((k,)), dma((k,)), dma((k,)),
             dma((4,)), dma((4,)), dma, dma, dma, dma, dma, dma,
             dma, dma, dma, dma,
         ],
         compiler_params=pltpu.CompilerParams(
-            collective_id=0, has_side_effects=True, vmem_limit_bytes=48 * 1024 * 1024
+            collective_id=0, has_side_effects=True, vmem_limit_bytes=40 * 1024 * 1024
         ),
-    )(snapshots, time_basis.T)
+    )(
+        pltpu.with_memory_space_constraint(snapshots, pltpu.HBM),
+        pltpu.with_memory_space_constraint(time_basis.T, pltpu.HBM),
+    )
 
 
 def solution(mesh):

time: 75.6 us -> 70.9 us (0.938)
  local copies, waits for them, and re-layouts: 4.77 us -> 1.98 us
  Pallas kernels: 70.1 us -> 68.2 us
    unnamed x7 -> x3, local copies, waits for them, and re-layouts: 4.77 us -> 1.98 us
    pallas_call x1, Pallas kernels: 70.1 us -> 68.2 us  [body(): pl.pallas_call(functools.partial(kernel, 1.0 / columns, 1.0 / (rank * poi...]
where the time goes in v3:
time: 70.9 us; the launch traced here: 70.8 us
  Pallas kernels  68.2 us (96%)
  local copies, waits for them, and re-layouts  1.98 us (3%)
    pallas_call x1, Pallas kernels, body(): pl.pallas_call(functools.partial(kernel, 1.0 / columns, 1.0 / (rank * poi...  68.2 us
    unnamed x3, local copies, waits for them, and re-layouts  1.98 us

profile of v3, /device:TPU:1, one launch (start us, length us, event | category | flops | bytes accessed | tf_op | source)
XLA Modules:
  0.0 70.8 jit_solution(4733532737462545521)
XLA Ops:
  0.6 68.2 %shard_map.49 = (f32[32,512]{1,0:T(8,128)S(1)}, f32[4,32,768]{2,1,0:T(8,128)S(1)}, f32[32,64]{1,0:T(8,128)S(1)}) custom-call(f32[32,32,768]{2,1,0:T(8,128)} %x_hbm.1, f32[64,512]{1,0:T(8,128)} %bitcast.1), custom_call_target="tpu_custom_call" | custom-call | tf_op jit(solution)/shard_map/pallas_call | solution.py:349
  68.8 0.6 copy.8
  69.4 0.7 %copy.9 = f32[4,32,768]{2,1,0:T(8,128)} copy(f32[4,32,768]{2,1,0:T(8,128)S(1)} %get-tuple-element.7) | data formatting | bytes 786432
  70.2 0.6 copy.10

commit v4 on v3

--- a/solution.py
+++ b/solution.py
@@ -35,12 +35,12 @@
 def kernel(
     scale_time, scale_param,
     x_hbm, basis_hbm, time_out, core_out, param_out,
-    basis_ref, staged, sent, mid, held, high_buf, low_buf, basis_high, basis_low,
-    gram, gram_sib, gram_sum, gram_in, rows_mine, rows_in, tiles,
+    basis_ref, staged, sent, mid, held, held_sib, high_buf, low_buf, basis_high, basis_low,
+    gram, gram_in, rows_mine, rows_in, tiles,
     core_sent, core_held, core_sib, pair_gram, pair_kept,
     part_mine, part_in, part_sum, part_z,
     relay, basis_sem, load_sem, x1_send, x1_recv, x2_send, x2_recv, c_send, c_recv, cs_send, cs_recv,
-    gs_send, gs_recv, g1_send, g1_recv, gz_send, gz_recv, gy_send, gy_recv,
+    f_send, f_recv, g1_send, g1_recv, gz_send, gz_recv, gy_send, gy_recv,
     px_send, px_recv, pz_send, pz_recv,
 ):
     sp, tm, me = lax.axis_index("space"), lax.axis_index("tm"), lax.axis_index("param")
@@ -164,27 +164,44 @@
         pair_gram[0] += (dot(high, low, NT) + dot(low, high, NT)) + dot(high, high, NT)
         pair_gram[1] += (dot(high, low_2, NT) + dot(low, high_2, NT)) + dot(high, high_2, NT)
 
+    def forward(k):
+        return remote(held.at[k], held_sib.at[k], f_send.at[k], f_recv.at[k], sibling)
+
+    def convert(blocks, k):
+        for pp in range(2):
+            high, low = split(blocks[k, pp].reshape(16, 2, 16, LANE))
+            high_buf[:, :, :, pp * LANE:(pp + 1) * LANE] = high
+            low_buf[:, :, :, pp * LANE:(pp + 1) * LANE] = low
+
+    def add_gram():
+        all_high = high_buf[...].reshape(512, 2 * LANE)
+        all_low = low_buf[...].reshape(512, 2 * LANE)
+        high = high_buf[:, me].reshape(256, 2 * LANE)
+        low = low_buf[:, me].reshape(256, 2 * LANE)
+        add = (dot(high, all_low, NT) + dot(low, all_high, NT)) + dot(high, all_high, NT)
+        add = add.reshape(16, 2, 8, 512)
+        gram[:, 0:2] += add[:, :, :, :256]
+        gram[:, 2:4] += add[:, :, :, 256:]
+
     for k in range(chunks):
         remote(
             mid.at[k, :, pl.ds(0, 3)], held.at[k, :, pl.ds(0, 3)],
             x2_send, x2_recv.at[k], sibling,
         ).wait_recv()
-        for pp in range(2):
-            high, low = split(held[k, pp].reshape(512, LANE))
-            high_buf[:, pp * LANE:(pp + 1) * LANE] = high
-            low_buf[:, pp * LANE:(pp + 1) * LANE] = low
+        forward(k).start()
+        convert(held, k)
         total = None
         for pp in range(2):
-            high = high_buf[:, pp * LANE:(pp + 1) * LANE]
-            low = low_buf[:, pp * LANE:(pp + 1) * LANE]
+            high = high_buf[:, :, :, pp * LANE:(pp + 1) * LANE].reshape(512, LANE)
+            low = low_buf[:, :, :, pp * LANE:(pp + 1) * LANE].reshape(512, LANE)
             term = (
                 dot(basis_high[pp], low, NN) + dot(basis_low[pp], high, NN)
             ) + dot(basis_high[pp], high, NN)
             total = term if total is None else total + term
         core_sent[k] = total.reshape(16, 8, LANE)
-        if 1 <= k <= 3:
+        if 1 <= k <= 4:
             pl.semaphore_wait(relay.at[k - 1], 2)
-        if k <= 2:
+        if k <= 3:
             pass_on(k)
         core_held[k, tm] = core_sent[k, tm]
         for dx, dy in ORDER:
@@ -192,36 +209,18 @@
             remote(
                 core_sent.at[k, to], core_held.at[k, tm], c_send, c_recv.at[k], (sp, to, me)
             ).start()
-        for dy in range(4):
-            there = lax.rem(y + dy, 4)
-            rows = pl.ds(pl.multiple_of(there * 128, 128), 128)
-            high, low = high_buf[rows, :], low_buf[rows, :]
-            add = (
-                dot(high, low_buf[...], NT) + dot(low, high_buf[...], NT)
-            ) + dot(high, high_buf[...], NT)
-            blocks = pl.ds(there * 4, 4)
-            gram[blocks] = gram[blocks] + add.reshape(4, 2, 16, 512)
-            if k == chunks - 1:
-                remote(
-                    gram.at[blocks, 1 - me], gram_sib.at[blocks],
-                    gs_send.at[dy], gs_recv.at[dy], sibling,
-                ).start()
-
-    for dy in range(4):
-        there = lax.rem(y + dy, 4)
-        blocks = pl.ds(there * 4, 4)
-        remote(
-            gram.at[blocks, 1 - me], gram_sib.at[blocks],
-            gs_send.at[dy], gs_recv.at[dy], sibling,
-        ).wait_recv()
-        gram_sum[blocks] = gram[blocks, me] + gram_sib[blocks]
-        for dx in (1, 3, 2, 0):
+        add_gram()
+        forward(k).wait_recv()
+        convert(held_sib, k)
+        add_gram()
+
+    for h in range(4):
+        for dx, dy in ORDER:
             to = peer(dx, dy)
-            if dx or dy:
-                remote(
-                    gram_sum.at[to], gram_in.at[tm], g1_send, g1_recv, (sp, to, me)
-                ).start()
-    gram_in[tm] = gram_sum[tm]
+            remote(
+                gram.at[to, h], gram_in.at[h, tm], g1_send, g1_recv.at[h], (sp, to, me)
+            ).start()
+        gram_in[h, tm] = gram[tm, h]
 
     for k in range(chunks):
         core_back(k)
@@ -250,18 +249,20 @@
         ).start()
     part_in[tm] = part_mine[...]
 
-    remote(
-        gram_sum.at[pl.ds(0, 15)], gram_in.at[pl.ds(0, 15)], g1_send, g1_recv, sibling
-    ).wait_recv()
-    rows = gram_in[0]
-    for j in range(1, 16):
-        rows = rows + gram_in[j]
-    rows_mine[...] = rows
-    for dz in far:
-        remote(
-            rows_mine, rows_in.at[sp], gz_send, gz_recv, (along(dz), tm, me)
-        ).start()
-    rows_in[sp] = rows
+    for h in range(4):
+        remote(
+            gram.at[pl.ds(0, 15), h], gram_in.at[h, pl.ds(0, 15)],
+            g1_send, g1_recv.at[h], sibling,
+        ).wait_recv()
+        rows = gram_in[h, 0]
+        for j in range(1, 16):
+            rows = rows + gram_in[h, j]
+        rows_mine[h] = rows
+        for dz in far + (0,):
+            remote(
+                rows_mine.at[h], rows_in.at[h, sp], gz_send, gz_recv.at[h],
+                (along(dz), tm, 1 - me),
+            ).start()
 
     remote(
         part_in.at[pl.ds(0, 15)], part_in.at[pl.ds(0, 15)], px_send, px_recv, sibling
@@ -278,14 +279,15 @@
     for k in range(chunks):
         core_write(k)
 
-    remote(
-        gram_in.at[pl.ds(0, 7)], rows_in.at[pl.ds(0, 7)], gz_send, gz_recv, sibling
-    ).wait_recv()
-    rows = rows_in[0]
-    for j in range(1, 8):
-        rows = rows + rows_in[j]
-    tiles[me] = rows * scale_time
-    swap = remote(tiles.at[me], tiles.at[me], gy_send, gy_recv, sibling)
+    for h in range(4):
+        remote(
+            gram_in.at[h, pl.ds(0, 8)], rows_in.at[h], gz_send, gz_recv.at[h], sibling
+        ).wait_recv()
+        rows = rows_in[h, 0]
+        for j in range(1, 8):
+            rows = rows + rows_in[h, j]
+        tiles[1 - me, (h % 2) * 8:(h % 2) * 8 + 8, (h // 2) * 256:(h // 2) * 256 + 256] = rows * scale_time
+    swap = remote(tiles.at[1 - me], tiles.at[1 - me], gy_send, gy_recv, sibling)
     swap.start()
 
     remote(
@@ -316,18 +318,12 @@
         remote(
             core_held.at[k], core_sib.at[k], cs_send.at[k], cs_recv.at[k], sibling
         ).wait_send()
-    for dy in range(4):
-        blocks = pl.ds(lax.rem(y + dy, 4) * 4, 4)
-        remote(
-            gram.at[blocks, 1 - me], gram_sib.at[blocks],
-            gs_send.at[dy], gs_recv.at[dy], sibling,
-        ).wait_send()
-    remote(
-        gram_sum.at[pl.ds(0, 15)], gram_in.at[pl.ds(0, 15)], g1_send, g1_recv, sibling
-    ).wait_send()
-    remote(
-        gram_in.at[pl.ds(0, 7)], rows_in.at[pl.ds(0, 7)], gz_send, gz_recv, sibling
-    ).wait_send()
+    for k in range(chunks):
+        forward(k).wait_send()
+    remote(
+        gram.at[pl.ds(0, 15)], gram.at[pl.ds(0, 15)], g1_send, g1_recv.at[0], sibling
+    ).wait_send()
+    remote(rows_in, rows_in, gz_send, gz_recv.at[0], sibling).wait_send()
     swap.wait_send()
     remote(
         part_in.at[pl.ds(0, 15)], part_in.at[pl.ds(0, 15)], px_send, px_recv, sibling
@@ -361,16 +357,15 @@
             vmem(block, f32),
             vmem(block, f32),
             vmem(block, f32),
-            vmem((512, 2 * LANE), bf16),
-            vmem((512, 2 * LANE), bf16),
+            vmem(block, f32),
+            vmem((16, 2, 16, 2 * LANE), bf16),
+            vmem((16, 2, 16, 2 * LANE), bf16),
             vmem((2, 128, 512), bf16),
             vmem((2, 128, 512), bf16),
-            vmem((16, 2, 16, 512), f32),
-            vmem((16, 16, 512), f32),
-            vmem((16, 16, 512), f32),
-            vmem((16, 16, 512), f32),
-            vmem((16, 512), f32),
-            vmem((8, 16, 512), f32),
+            vmem((16, 4, 8, 256), f32),
+            vmem((4, 16, 8, 256), f32),
+            vmem((4, 8, 256), f32),
+            vmem((4, 8, 8, 256), f32),
             vmem((2, 16, 512), f32),
             vmem((k, 16, 8, LANE), f32),
             vmem((k, 16, 8, LANE), f32),
@@ -381,9 +376,9 @@
             vmem((16, 16, LANE), f32),
             vmem((16, LANE), f32),
             vmem((8, 16, LANE), f32),
-            pltpu.SemaphoreType.REGULAR((3,)),
+            pltpu.SemaphoreType.REGULAR((4,)),
             dma, dma((k,)), dma, dma((k, 2)), dma, dma((k,)), dma, dma((k,)), dma((k,)), dma((k,)),
-            dma((4,)), dma((4,)), dma, dma, dma, dma, dma, dma,
+            dma((k,)), dma((k,)), dma, dma((4,)), dma, dma((4,)), dma, dma,
             dma, dma, dma, dma,
         ],
         compiler_params=pltpu.CompilerParams(

time: 70.9 us -> 68.1 us (0.961)
  Pallas kernels: 68.2 us -> 65.4 us
    pallas_call x1, Pallas kernels: 68.2 us -> 65.4 us  [body(): pl.pallas_call(functools.partial(kernel, 1.0 / columns, 1.0 / (rank * poi...]
where the time goes in v4:
time: 68.1 us; the launch traced here: 68 us
  Pallas kernels  65.4 us (96%)
  local copies, waits for them, and re-layouts  1.98 us (3%)
    pallas_call x1, Pallas kernels, body(): pl.pallas_call(functools.partial(kernel, 1.0 / columns, 1.0 / (rank * poi...  65.4 us
    unnamed x3, local copies, waits for them, and re-layouts  1.98 us

profile of v4, /device:TPU:1, one launch (start us, length us, event | category | flops | bytes accessed | tf_op | source)
XLA Modules:
  0.0 68.0 jit_solution(16161812721552309257)
XLA Ops:
  0.6 65.4 %shard_map.49 = (f32[32,512]{1,0:T(8,128)S(1)}, f32[4,32,768]{2,1,0:T(8,128)S(1)}, f32[32,64]{1,0:T(8,128)S(1)}) custom-call(f32[32,32,768]{2,1,0:T(8,128)} %x_hbm.1, f32[64,512]{1,0:T(8,128)} %bitcast.1), custom_call_target="tpu_custom_call" | custom-call | tf_op jit(solution)/shard_map/pallas_call | solution.py:345
  66.1 0.6 copy.8
  66.7 0.7 %copy.9 = f32[4,32,768]{2,1,0:T(8,128)} copy(f32[4,32,768]{2,1,0:T(8,128)S(1)} %get-tuple-element.7) | data formatting | bytes 786432
  67.4 0.6 copy.10

commit v5 on v4

--- a/solution.py
+++ b/solution.py
@@ -333,6 +333,17 @@
     ).wait_send()
 
 
+def write(a, b, c, x, y, z, sem):
+    copies = [
+        pltpu.make_async_copy(src, dst, sem.at[i])
+        for i, (src, dst) in enumerate(((b, y), (a, x), (c, z)))
+    ]
+    for copy in copies:
+        copy.start()
+    for copy in copies:
+        copy.wait()
+
+
 def body(snapshots, time_basis):
     f32, bf16 = jnp.float32, jnp.bfloat16
     time_local, load_local, point_local = snapshots.shape
@@ -342,7 +353,7 @@
     vmem = pltpu.VMEM
     dma = pltpu.SemaphoreType.DMA
     block = (k, 2, 4, 4, time_local, LANE)
-    return pl.pallas_call(
+    outs = pl.pallas_call(
         functools.partial(kernel, 1.0 / columns, 1.0 / (rank * point_local * 8)),
         out_shape=(
             jax.ShapeDtypeStruct((32, 512), f32),
@@ -388,6 +399,14 @@
         pltpu.with_memory_space_constraint(snapshots, pltpu.HBM),
         pltpu.with_memory_space_constraint(time_basis.T, pltpu.HBM),
     )
+    return pl.pallas_call(
+        write,
+        out_shape=tuple(jax.ShapeDtypeStruct(v.shape, v.dtype) for v in outs),
+        in_specs=[pl.BlockSpec(memory_space=vmem)] * 3,
+        out_specs=(pl.BlockSpec(memory_space=pl.ANY),) * 3,
+        scratch_shapes=[dma((3,))],
+        compiler_params=pltpu.CompilerParams(vmem_limit_bytes=4 * 1024 * 1024),
+    )(*outs)
 
 
 def solution(mesh):

time: 68.1 us -> 66.9 us (0.982)
  local copies, waits for them, and re-layouts: 1.98 us -> 0 us
  Pallas kernels: 65.4 us -> 66.2 us
    unnamed x3 -> x0, local copies, waits for them, and re-layouts: 1.98 us -> none
    pallas_call x0 -> x1, Pallas kernels: none -> 0.79 us  [body(): pl.pallas_call(write, out_shape=tuple((jax.ShapeDtypeStruct(v.shape, v.dt...]
where the time goes in v5:
time: 66.9 us; the launch traced here: 66.8 us
  Pallas kernels  66.2 us (99%)
    pallas_call x1, Pallas kernels, body(): pl.pallas_call(functools.partial(kernel, 1.0 / columns, 1.0 / (rank * poi...  65.4 us

profile of v5, /device:TPU:1, one launch (start us, length us, event | category | flops | bytes accessed | tf_op | source)
XLA Modules:
  0.0 66.8 jit_solution(12184869150443863546)
XLA Ops:
  0.6 65.4 %shard_map.49 = (f32[32,512]{1,0:T(8,128)S(1)}, f32[4,32,768]{2,1,0:T(8,128)S(1)}, f32[32,64]{1,0:T(8,128)S(1)}) custom-call(f32[32,32,768]{2,1,0:T(8,128)} %x_hbm.1, f32[64,512]{1,0:T(8,128)} %bitcast.1), custom_call_target="tpu_custom_call" | custom-call | tf_op jit(solution)/shard_map/pallas_call | solution.py:356
  66.1 0.8 %shard_map.50 = (f32[32,512]{1,0:T(8,128)}, f32[4,32,768]{2,1,0:T(8,128)}, f32[32,64]{1,0:T(8,128)}) custom-call(f32[32,512]{1,0:T(8,128)S(1)} %get-tuple-element.6.a, f32[4,32,768]{2,1,0:T(8,128)S(1)} %get-tuple-element.7.b, f32[32,64]{1,0:T(8,128)S(1)} %get-tuple-element.8.c), custom_call_target="tpu_custom_call" | custom-call | tf_op jit(solution)/shard_map/pallas_call | solution.py:402

commit v6 on v5

--- a/solution.py
+++ b/solution.py
@@ -204,7 +204,7 @@
         if k <= 3:
             pass_on(k)
         core_held[k, tm] = core_sent[k, tm]
-        for dx, dy in ORDER:
+        for dx, dy in ORDER[::-1]:
             to = peer(dx, dy)
             remote(
                 core_sent.at[k, to], core_held.at[k, tm], c_send, c_recv.at[k], (sp, to, me)
@@ -215,17 +215,40 @@
         add_gram()
 
     for h in range(4):
-        for dx, dy in ORDER:
+        for dx, dy in ORDER[::-1]:
             to = peer(dx, dy)
             remote(
                 gram.at[to, h], gram_in.at[h, tm], g1_send, g1_recv.at[h], (sp, to, me)
             ).start()
         gram_in[h, tm] = gram[tm, h]
 
-    for k in range(chunks):
+    def spread(h):
+        remote(
+            gram.at[pl.ds(0, 15), h], gram_in.at[h, pl.ds(0, 15)],
+            g1_send, g1_recv.at[h], sibling,
+        ).wait_recv()
+        rows = gram_in[h, 0]
+        for j in range(1, 16):
+            rows = rows + gram_in[h, j]
+        rows_mine[h] = rows
+        for dz in far + (0,):
+            remote(
+                rows_mine.at[h], rows_in.at[h, sp], gz_send, gz_recv.at[h],
+                (along(dz), tm, 1 - me),
+            ).start()
+
+    for k in range(0, chunks - 1):
         core_back(k)
-    for k in range(chunks):
+    for k in range(0, chunks - 2):
         core_pair(k)
+    for h in range(0, 1):
+        spread(h)
+    for k in range(chunks - 1, chunks):
+        core_back(k)
+    for k in range(chunks - 2, chunks):
+        core_pair(k)
+    for h in range(1, 2):
+        spread(h)
     row = lax.broadcasted_iota(jnp.int32, (128, 128), 0)
     col = lax.broadcasted_iota(jnp.int32, (128, 128), 1)
     same = lax.rem(row, 4) == lax.rem(col, 4)
@@ -249,20 +272,8 @@
         ).start()
     part_in[tm] = part_mine[...]
 
-    for h in range(4):
-        remote(
-            gram.at[pl.ds(0, 15), h], gram_in.at[h, pl.ds(0, 15)],
-            g1_send, g1_recv.at[h], sibling,
-        ).wait_recv()
-        rows = gram_in[h, 0]
-        for j in range(1, 16):
-            rows = rows + gram_in[h, j]
-        rows_mine[h] = rows
-        for dz in far + (0,):
-            remote(
-                rows_mine.at[h], rows_in.at[h, sp], gz_send, gz_recv.at[h],
-                (along(dz), tm, 1 - me),
-            ).start()
+    for h in range(2, 4):
+        spread(h)
 
     remote(
         part_in.at[pl.ds(0, 15)], part_in.at[pl.ds(0, 15)], px_send, px_recv, sibling

time: 66.9 us -> 66.3 us (level)
  Pallas kernels: 66.2 us -> 65.5 us
    pallas_call x1, Pallas kernels: 65.4 us -> 64.7 us  [body(): pl.pallas_call(functools.partial(kernel, 1.0 / columns, 1.0 / (rank * poi...]
where the time goes in v6:
time: 66.3 us; the launch traced here: 66.2 us
  Pallas kernels  65.5 us (99%)
    pallas_call x1, Pallas kernels, body(): pl.pallas_call(functools.partial(kernel, 1.0 / columns, 1.0 / (rank * poi...  64.7 us

profile of v6, /device:TPU:1, one launch (start us, length us, event | category | flops | bytes accessed | tf_op | source)
XLA Modules:
  0.0 66.2 jit_solution(5199422300039974277)
XLA Ops:
  0.6 64.7 %shard_map.49 = (f32[32,512]{1,0:T(8,128)S(1)}, f32[4,32,768]{2,1,0:T(8,128)S(1)}, f32[32,64]{1,0:T(8,128)S(1)}) custom-call(f32[32,32,768]{2,1,0:T(8,128)} %x_hbm.1, f32[64,512]{1,0:T(8,128)} %bitcast.1), custom_call_target="tpu_custom_call" | custom-call | tf_op jit(solution)/shard_map/pallas_call | solution.py:367
  65.4 0.8 %shard_map.50 = (f32[32,512]{1,0:T(8,128)}, f32[4,32,768]{2,1,0:T(8,128)}, f32[32,64]{1,0:T(8,128)}) custom-call(f32[32,512]{1,0:T(8,128)S(1)} %get-tuple-element.6.a, f32[4,32,768]{2,1,0:T(8,128)S(1)} %get-tuple-element.7.b, f32[32,64]{1,0:T(8,128)S(1)} %get-tuple-element.8.c), custom_call_target="tpu_custom_call" | custom-call | tf_op jit(solution)/shard_map/pallas_call | solution.py:413

commit v7 on v6

--- a/solution.py
+++ b/solution.py
@@ -60,7 +60,7 @@
         )
 
     sibling = (sp, tm, 1 - me)
-    ring = (1, 3, 2)
+    ring = (2, 1, 3)
     far = (4, 3, 5, 2, 6, 1, 7)
 
     def load(k):

time: 66.3 us -> 65.9 us (level)
  no operation moved by 1% of the time
where the time goes in v7:
time: 65.9 us; the launch traced here: 65.8 us
  Pallas kernels  65.2 us (99%)
    pallas_call x1, Pallas kernels, body(): pl.pallas_call(functools.partial(kernel, 1.0 / columns, 1.0 / (rank * poi...  64.4 us

profile of v7, /device:TPU:1, one launch (start us, length us, event | category | flops | bytes accessed | tf_op | source)
XLA Modules:
  0.0 65.8 jit_solution(3818741041153781320)
XLA Ops:
  0.6 64.4 %shard_map.49 = (f32[32,512]{1,0:T(8,128)S(1)}, f32[4,32,768]{2,1,0:T(8,128)S(1)}, f32[32,64]{1,0:T(8,128)S(1)}) custom-call(f32[32,32,768]{2,1,0:T(8,128)} %x_hbm.1, f32[64,512]{1,0:T(8,128)} %bitcast.1), custom_call_target="tpu_custom_call" | custom-call | tf_op jit(solution)/shard_map/pallas_call | solution.py:367
  65.0 0.8 %shard_map.50 = (f32[32,512]{1,0:T(8,128)}, f32[4,32,768]{2,1,0:T(8,128)}, f32[32,64]{1,0:T(8,128)}) custom-call(f32[32,512]{1,0:T(8,128)S(1)} %get-tuple-element.6.a, f32[4,32,768]{2,1,0:T(8,128)S(1)} %get-tuple-element.7.b, f32[32,64]{1,0:T(8,128)S(1)} %get-tuple-element.8.c), custom_call_target="tpu_custom_call" | custom-call | tf_op jit(solution)/shard_map/pallas_call | solution.py:413
